TPU v7x, 32 devices: a whole 2x2x4 slice. The times are simulated.
32 devices in a mesh: grp: 2 (over y), tm: 8 (over z, x), row: 2 (over core).
Axes of the slice: x: 2, y: 2, z: 4, core: 2. Of those that a mesh axis runs over, the one named last changes fastest.
Arguments:
- queries: bfloat16 [4096, 768], P(('grp', 'tm', 'row')), parts along dimension 0, may hold values from -5 to 5
- keys: bfloat16 [4096, 768], P(('grp', 'tm', 'row')), parts along dimension 0, may hold values from -5 to 5
- values: bfloat16 [4096, 768], P(('grp', 'tm', 'row')), parts along dimension 0, may hold values from -6 to 6
- d_out: bfloat16 [4096, 768], P(('grp', 'tm', 'row')), parts along dimension 0, may hold values from -6 to 6
- action_table: bfloat16 [8, 768], replicated, may hold values from -5 to 5
- actions: int32 [16], P(('grp', 'tm')), parts along dimension 0, may hold values from 0 to 7
- temporal_list: int32 [32, 2], P(('grp', 'tm', 'row')), parts along dimension 0, may hold values from 1 to 3, as said below
Outputs:
- attended: bfloat16 [4096, 768], P(('grp', 'tm', 'row')), parts along dimension 0
- grad_queries: bfloat16 [4096, 768], P(('grp', 'tm', 'row')), parts along dimension 0
- grad_keys: bfloat16 [4096, 768], P(('grp', 'tm', 'row')), parts along dimension 0
- grad_values: bfloat16 [4096, 768], P(('grp', 'tm', 'row')), parts along dimension 0
- grad_table: float32 [16, 768], P('grp'), parts along dimension 0
There are 2 independent parts, one for each index of `grp`. A program takes and returns all parts, laid end to end along the dimension named above; an argument that names none is the same for every part. Nothing has to cross between parts.
Inputs may be any that keep to these rules, and one draw needn't show every extreme that they name: `temporal_list`: row b lists, in rising order, 2 different frame distances of 1 to 3.
All inputs are finite; a program needn't handle non-finite values.
Results may differ from a plain program's by a relative error of at most 0.012.
Values may be sent and summed in bfloat16 or wider, within the bound.
No kernel may reach another device: no remote copies, remote signals or barrier semaphores. Data moves between devices by JAX's collectives and lax.ppermute only.
A program may use at most 64 MiB of HBM per device.

v0:
```python
import math
import jax
import jax.numpy as jnp
from jax import lax
from jax.sharding import PartitionSpec as P

HEADS = 8
HEAD_DIM = 96
DIST = 3
LIST = 2


def from_behind(block, axis, distance):
    devices = range(lax.axis_size(axis))
    route = [(i - distance, i) for i in devices if i - distance in devices]
    return lax.ppermute(block, axis, route)


def attention_pass(queries, key_set, value_set, allowed, d_out):
    query_rows = queries.shape[0]
    key_rows = key_set.shape[0]
    model_width = queries.shape[1]
    score_scale = 1.0 / math.sqrt(HEAD_DIM)
    query_heads = queries.reshape(query_rows, HEADS, HEAD_DIM)
    key_heads = key_set.reshape(key_rows, HEADS, HEAD_DIM)
    value_heads = value_set.reshape(key_rows, HEADS, HEAD_DIM)
    grad_heads = d_out.reshape(query_rows, HEADS, HEAD_DIM)
    scores = (
        jnp.einsum("qhd,khd->hqk", query_heads, key_heads, preferred_element_type=jnp.float32)
        * score_scale
    )
    scores = jnp.where(allowed[None, None, :], scores, -1e30)
    highest = jnp.max(scores, axis=2, keepdims=True)
    weights = jnp.where(allowed[None, None, :], jnp.exp(scores - highest), 0.0)
    totals = jnp.sum(weights, axis=2, keepdims=True)
    probabilities = weights / totals
    log_total = (highest + jnp.log(totals))[:, :, 0].T
    probs_low = probabilities.astype(jnp.bfloat16)
    out_full = jnp.einsum(
        "hqk,khd->qhd", probs_low, value_heads, preferred_element_type=jnp.float32
    )
    d_probs = jnp.einsum(
        "qhd,khd->hqk", grad_heads, value_heads, preferred_element_type=jnp.float32
    )
    centre = jnp.sum(grad_heads.astype(jnp.float32) * out_full, axis=2)
    d_scores = (probabilities * (d_probs - centre.T[:, :, None])).astype(jnp.bfloat16)
    grad_query = (
        jnp.einsum("hqk,khd->qhd", d_scores, key_heads, preferred_element_type=jnp.float32)
        * score_scale
    )
    grad_key = None
    grad_value = None
    grad_key = (
        jnp.einsum(
            "hqk,qhd->khd", d_scores, query_heads, preferred_element_type=jnp.float32
        ).reshape(key_rows, model_width)
        * score_scale
    )
    grad_value = jnp.einsum(
        "hqk,qhd->khd", probs_low, grad_heads, preferred_element_type=jnp.float32
    ).reshape(key_rows, model_width)
    return (
        out_full.reshape(query_rows, model_width),
        grad_query.reshape(query_rows, model_width),
        grad_key,
        grad_value,
        log_total,
        centre,
    )


def on_device(queries, keys, values, d_out, action_table, actions, temporal_list):
    block_rows = queries.shape[0]
    model_width = queries.shape[1]
    frame_index = lax.axis_index("tm")
    labels = lax.iota(jnp.int32, action_table.shape[0])
    matches = actions[0] == labels
    action_row = jnp.dot(
        matches.astype(jnp.bfloat16)[None, :], action_table, preferred_element_type=jnp.float32
    )
    cond_values = (values.astype(jnp.float32) + action_row).astype(jnp.bfloat16)
    own_pair = jnp.stack([keys, cond_values])
    frame_pair = lax.all_gather(own_pair, "row", axis=1, tiled=True)
    earlier = []
    moving = own_pair
    for distance in range(DIST):
        moving = from_behind(moving, "tm", 1)
        earlier.append(moving)
    stacked = jnp.stack(earlier)
    distances = temporal_list[0]
    chosen = jnp.take(stacked, distances - 1, axis=0)
    frame_tokens = frame_pair.shape[1]
    key_set = jnp.concatenate(
        [frame_pair[0], chosen[:, 0].reshape(LIST * block_rows, model_width)], axis=0
    )
    value_set = jnp.concatenate(
        [frame_pair[1], chosen[:, 1].reshape(LIST * block_rows, model_width)], axis=0
    )
    present = frame_index - distances >= 0
    allowed = jnp.concatenate(
        [jnp.ones((frame_tokens,), dtype=bool), jnp.repeat(present, block_rows)]
    )
    out_full, grad_query, grad_key, grad_value, log_total, centre = attention_pass(
        queries, key_set, value_set, allowed, d_out
    )
    frame_terms = jnp.stack([grad_key[:frame_tokens], grad_value[:frame_tokens]])
    frame_grads = lax.psum_scatter(frame_terms, "row", scatter_dimension=1, tiled=True)
    slot_grads = []
    for listed in range(LIST):
        first_row = frame_tokens + listed * block_rows
        slot_grads.append(
            jnp.stack(
                [
                    grad_key[first_row : first_row + block_rows],
                    grad_value[first_row : first_row + block_rows],
                ]
            )
        )
    partials = []
    for distance in range(DIST):
        summed = jnp.zeros((2, block_rows, model_width), jnp.float32)
        for listed in range(LIST):
            summed = summed + jnp.where(distances[listed] == distance + 1, slot_grads[listed], 0.0)
        partials.append(summed)
    carried = jnp.zeros_like(partials[0])
    for distance in reversed(range(DIST)):
        carried = from_behind(carried + partials[distance], "tm", -1)
    key_total = frame_grads[0] + carried[0]
    value_total = frame_grads[1] + carried[1]
    column_sums = jnp.sum(value_total, axis=0)
    local_table = jnp.where(matches[:, None], column_sums[None, :], 0.0)
    grad_table = lax.psum(local_table, ("tm", "row"))
    return (
        out_full.astype(jnp.bfloat16),
        grad_query.astype(jnp.bfloat16),
        key_total.astype(jnp.bfloat16),
        value_total.astype(jnp.bfloat16),
        grad_table,
    )


def solution(mesh):
    return jax.shard_map(
        on_device,
        mesh=mesh,
        in_specs=(
            P(("grp", "tm", "row"), None),
            P(("grp", "tm", "row"), None),
            P(("grp", "tm", "row"), None),
            P(("grp", "tm", "row"), None),
            P(),
            P(("grp", "tm")),
            P(("grp", "tm", "row"), None),
        ),
        out_specs=(
            P(("grp", "tm", "row"), None),
            P(("grp", "tm", "row"), None),
            P(("grp", "tm", "row"), None),
            P(("grp", "tm", "row"), None),
            P("grp", None),
        ),
        check_vma=False,
    )
```

profile of v0, /device:TPU:0, one launch (start us, length us, event | category | flops | bytes accessed | tf_op | source)
XLA Modules:
  0.0 186.7 jit_solution(2967923302324929908)
XLA Ops:
  8.1 1.0 fusion.14
  10.1 4.9 %collective-permute-start = (bf16[2,128,768]{2,1,0:T(8,128)(2,1)S(1)}, bf16[2,128,768]{2,1,0:T(8,128)(2,1)S(1)}, u32[]{:S(2)}, u32[]{:S(2)}) collective-permute-start(bf16[2,128,768]{2,1,0:T(8,128)(2,1)S(1)} %pad_maximum_fusion.10), channel_id=1, source_target_pairs={{0,2},{2,4},{4,6},{6,8},{8,10},{10,12},{12,14},{1,3},{3,5},{5,7},{... | collective-permute-start | bytes 1179656 | tf_op jit(solution)/shard_map/ppermute | solution.py:16
  16.4 6.9 %collective-permute-done = bf16[2,128,768]{2,1,0:T(8,128)(2,1)S(1)} collective-permute-done((bf16[2,128,768]{2,1,0:T(8,128)(2,1)S(1)}, bf16[2,128,768]{2,1,0:T(8,128)(2,1)S(1)}, u32[]{:S(2)}, u32[]{:S(2)}) %collective-permute-start) | collective-permute-done | bytes 393248 | tf_op jit(solution)/shard_map/ppermute | solution.py:16
  23.3 4.4 %collective-permute-start.1 = (bf16[2,128,768]{2,1,0:T(8,128)(2,1)S(1)}, bf16[2,128,768]{2,1,0:T(8,128)(2,1)S(1)}, u32[]{:S(2)}, u32[]{:S(2)}) collective-permute-start(bf16[2,128,768]{2,1,0:T(8,128)(2,1)S(1)} %collective-permute-done), channel_id=1, source_target_pairs={{0,2},{2,4},{4,6},{6,8},{8,10},{10,12},{12,14},{1,3},{3,5},{5,7},{... | collective-permute-start | bytes 1179656 | tf_op jit(solution)/shard_map/ppermute | solution.py:16
  27.7 2.4 %all_gather.3 = bf16[2,256,768]{2,1,0:T(8,128)(2,1)S(1)} all-gather(bf16[2,128,768]{2,1,0:T(8,128)(2,1)S(1)} %pad_maximum_fusion.10), channel_id=1, replica_groups=mesh['grp'=2,'tm'=8,'row'=2] {'row'}, dimensions={1}, use_global_device_ids=true | all-gather | bytes 1179648 | tf_op jit(solution)/shard_map/all_gather | solution.py:83
  30.1 5.0 %collective-permute-done.1 = bf16[2,128,768]{2,1,0:T(8,128)(2,1)S(1)} collective-permute-done((bf16[2,128,768]{2,1,0:T(8,128)(2,1)S(1)}, bf16[2,128,768]{2,1,0:T(8,128)(2,1)S(1)}, u32[]{:S(2)}, u32[]{:S(2)}) %collective-permute-start.1) | collective-permute-done | bytes 393248 | tf_op jit(solution)/shard_map/ppermute | solution.py:16
  35.2 5.1 %collective-permute-start.2 = (bf16[2,128,768]{2,1,0:T(8,128)(2,1)S(1)}, bf16[2,128,768]{2,1,0:T(8,128)(2,1)}, u32[]{:S(2)}, u32[]{:S(2)}) collective-permute-start(bf16[2,128,768]{2,1,0:T(8,128)(2,1)S(1)} %collective-permute-done.1), channel_id=1, source_target_pairs={{0,2},{2,4},{4,6},{6,8},{8,10},{10,12},{12,14},{1,3},{3,5},{5,7},{... | collective-permute-start | bytes 1179656 | tf_op jit(solution)/shard_map/ppermute | solution.py:16
  43.6 2.5 %collective-permute-done.2 = bf16[2,128,768]{2,1,0:T(8,128)(2,1)} collective-permute-done((bf16[2,128,768]{2,1,0:T(8,128)(2,1)S(1)}, bf16[2,128,768]{2,1,0:T(8,128)(2,1)}, u32[]{:S(2)}, u32[]{:S(2)}) %collective-permute-start.2) | collective-permute-done | bytes 393248 | tf_op jit(solution)/shard_map/ppermute | solution.py:16
  46.1 1.1 pad_maximum_fusion.1
  50.8 1.6 convolution_bitcast_fusion
  52.5 1.1 multiply_reduce_fusion
  55.7 1.0 fusion.27
  57.6 1.2 pad_maximum_fusion
  58.9 1.4 copy-done.2
  61.2 1.3 collective-permute-start.3
  63.8 17.5 %collective-permute-done.3 = f32[2,128,768]{2,1,0:T(8,128)S(1)} collective-permute-done((f32[2,128,768]{2,1,0:T(8,128)S(1)}, f32[2,128,768]{2,1,0:T(8,128)S(1)}, u32[]{:S(2)}, u32[]{:S(2)}) %collective-permute-start.3) | collective-permute-done | bytes 786464 | tf_op jit(solution)/shard_map/ppermute | solution.py:16
  81.4 1.4 collective-permute-start.4
  84.2 17.0 %collective-permute-done.4 = f32[2,128,768]{2,1,0:T(8,128)S(1)} collective-permute-done((f32[2,128,768]{2,1,0:T(8,128)S(1)}, f32[2,128,768]{2,1,0:T(8,128)S(1)}, u32[]{:S(2)}, u32[]{:S(2)}) %collective-permute-start.4) | collective-permute-done | bytes 786464 | tf_op jit(solution)/shard_map/ppermute | solution.py:16
  101.1 1.0 add_add_fusion
  102.2 1.3 collective-permute-start.5
  103.5 1.7 copy.47
  106.4 13.7 %collective-permute-done.5 = f32[2,128,768]{2,1,0:T(8,128)S(1)} collective-permute-done((f32[2,128,768]{2,1,0:T(8,128)}, f32[2,128,768]{2,1,0:T(8,128)S(1)}, u32[]{:S(2)}, u32[]{:S(2)}) %collective-permute-start.5) | collective-permute-done | bytes 786464 | tf_op jit(solution)/shard_map/ppermute | solution.py:16
  120.1 2.0 %fusion.16 = (f32[768]{0:T(1024)S(1)}, bf16[128,768]{1,0:T(8,128)(2,1)}, bf16[128,768]{1,0:T(8,128)(2,1)}) fusion(f32[2,128,768]{2,1,0:T(8,128)S(1)} %collective-permute-done.5, f32[2,128,768]{2,1,0:T(8,128)} %reduce-scatter.2.cloned.1.call-done), kind=kLoop, calls=%fused_computation.41 | loop fusion | flops 490752 | bytes 1969152 | tf_op jit(solution)/shard_map/reduce_sum | solution.py:130
  122.2 57.6 %psum.7 = f32[8,768]{1,0:T(8,128)} all-reduce(f32[8,768]{1,0:T(8,128)S(1)} %broadcast_select_fusion.1), channel_id=1, replica_groups=mesh['grp'=2,'tm'=8,'row'=2] {'tm','row'}, use_global_device_ids=true, to_apply=%region_5.6 | all-reduce | flops 6144 | bytes 49152 | tf_op jit(solution)/shard_map/psum | solution.py:132
  (68 shorter events, 13.5 us)
Async XLA Ops:
  7.2 0.8 copy-start
  7.2 33.1 %copy-start.12 = (s32[1,2]{1,0:T(1,128)S(1)}, s32[1,2]{1,0:T(1,128)}, u32[]{:S(2)}) copy-start(s32[1,2]{1,0:T(1,128)} %param.13) | copy-start | bytes 28
  7.2 35.0 %copy-start.10 = (bf16[128,768]{1,0:T(8,128)(2,1)S(1)}, bf16[128,768]{1,0:T(8,128)(2,1)}, u32[]{:S(2)}) copy-start(bf16[128,768]{1,0:T(8,128)(2,1)} %param.7) | copy-start | bytes 589828
  7.2 112.9 %reduce-scatter.2.cloned.1.call-start = ((), (), s32[]{:S(2)}) async-start(), calls=%async_computation.1 | async-start | bytes 2359296 | tf_op jit(solution)/shard_map/reduce_scatter | solution.py:107
  8.1 34.2 %copy-start.11 = (bf16[128,768]{1,0:T(8,128)(2,1)S(1)}, bf16[128,768]{1,0:T(8,128)(2,1)}, u32[]{:S(2)}) copy-start(bf16[128,768]{1,0:T(8,128)(2,1)} %param.10) | copy-start | bytes 589828
  10.1 13.2 %collective-permute-start = (bf16[2,128,768]{2,1,0:T(8,128)(2,1)S(1)}, bf16[2,128,768]{2,1,0:T(8,128)(2,1)S(1)}, u32[]{:S(2)}, u32[]{:S(2)}) collective-permute-start(bf16[2,128,768]{2,1,0:T(8,128)(2,1)S(1)} %pad_maximum_fusion.10), channel_id=1, source_target_pairs={{0,2},{2,4},{4,6},{6,8},{8,10},{10,12},{12,14},{1,3},{3,5},{5,7},{... | collective-permute-start | bytes 1179656 | tf_op jit(solution)/shard_map/ppermute | solution.py:16
  23.3 11.9 %collective-permute-start.1 = (bf16[2,128,768]{2,1,0:T(8,128)(2,1)S(1)}, bf16[2,128,768]{2,1,0:T(8,128)(2,1)S(1)}, u32[]{:S(2)}, u32[]{:S(2)}) collective-permute-start(bf16[2,128,768]{2,1,0:T(8,128)(2,1)S(1)} %collective-permute-done), channel_id=1, source_target_pairs={{0,2},{2,4},{4,6},{6,8},{8,10},{10,12},{12,14},{1,3},{3,5},{5,7},{... | collective-permute-start | bytes 1179656 | tf_op jit(solution)/shard_map/ppermute | solution.py:16
  35.2 10.9 %collective-permute-start.2 = (bf16[2,128,768]{2,1,0:T(8,128)(2,1)S(1)}, bf16[2,128,768]{2,1,0:T(8,128)(2,1)}, u32[]{:S(2)}, u32[]{:S(2)}) collective-permute-start(bf16[2,128,768]{2,1,0:T(8,128)(2,1)S(1)} %collective-permute-done.1), channel_id=1, source_target_pairs={{0,2},{2,4},{4,6},{6,8},{8,10},{10,12},{12,14},{1,3},{3,5},{5,7},{... | collective-permute-start | bytes 1179656 | tf_op jit(solution)/shard_map/ppermute | solution.py:16
  48.7 1.2 copy-start.3
  50.8 1.6 copy-start.9
  54.1 1.0 copy-start.7
  55.6 1.7 copy-start.1
  58.9 1.4 copy-start.2
  58.9 1.5 copy-start.6
  58.9 1.7 copy-start.5
  61.2 20.1 %collective-permute-start.3 = (f32[2,128,768]{2,1,0:T(8,128)S(1)}, f32[2,128,768]{2,1,0:T(8,128)S(1)}, u32[]{:S(2)}, u32[]{:S(2)}) collective-permute-start(f32[2,128,768]{2,1,0:T(8,128)S(1)} %select_add_fusion), channel_id=1, source_target_pairs={{2,0},{4,2},{6,4},{8,6},{10,8},{12,10},{14,12},{3,1},{5,3},{7,5},{... | collective-permute-start | bytes 2359304 | tf_op jit(solution)/shard_map/ppermute | solution.py:16
  81.4 23.8 %copy-start.4 = (bf16[256,8,96]{0,2,1:T(8,128)(2,1)S(1)}, bf16[256,8,96]{0,2,1:T(8,128)(2,1)}, u32[]{:S(2)}) copy-start(bf16[256,8,96]{0,2,1:T(8,128)(2,1)} %copy-done.3) | copy-start | bytes 1179652
  81.4 23.8 %copy-start.8 = (bf16[8,128,512]{1,2,0:T(8,128)(2,1)S(1)}, bf16[8,128,512]{1,2,0:T(8,128)(2,1)}, u32[]{:S(2)}) copy-start(bf16[8,128,512]{1,2,0:T(8,128)(2,1)} %copy-done.7) | copy-start | bytes 3145732
  81.4 19.7 %collective-permute-start.4 = (f32[2,128,768]{2,1,0:T(8,128)S(1)}, f32[2,128,768]{2,1,0:T(8,128)S(1)}, u32[]{:S(2)}, u32[]{:S(2)}) collective-permute-start(f32[2,128,768]{2,1,0:T(8,128)S(1)} %add_add_fusion.1), channel_id=1, source_target_pairs={{2,0},{4,2},{6,4},{8,6},{10,8},{12,10},{14,12},{3,1},{5,3},{7,5},{... | collective-permute-start | bytes 2359304 | tf_op jit(solution)/shard_map/ppermute | solution.py:16
  102.2 18.0 %collective-permute-start.5 = (f32[2,128,768]{2,1,0:T(8,128)}, f32[2,128,768]{2,1,0:T(8,128)S(1)}, u32[]{:S(2)}, u32[]{:S(2)}) collective-permute-start(f32[2,128,768]{2,1,0:T(8,128)} %add_add_fusion), channel_id=1, source_target_pairs={{2,0},{4,2},{6,4},{8,6},{10,8},{12,10},{14,12},{3,1},{5,3},{7,5},{... | collective-permute-start | bytes 2359304 | tf_op jit(solution)/shard_map/ppermute | solution.py:16
Sparse Core Ops, SparseCore 0:
  59.0 13.1 reduce-scatter.1
where the time goes:
time: 187 us
  waiting for transfers between devices  62.6 us (33%)
  blocking collectives  60 us (32%)
  between operations  19 us (10%)
  starting transfers between devices  18.4 us (10%)
  local copies, waits for them, and re-layouts  11.8 us (6%)
  other arithmetic  10 us (5%)
  matrix products  4.76 us (3%)
    ppermute x6, waiting for transfers between devices, from_behind(): return lax.ppermute(block, axis, route)  62.6 us
    psum x1, blocking collectives, on_device(): grad_table = lax.psum(local_table, ('tm', 'row'))  57.6 us
    ppermute x6, starting transfers between devices, from_behind(): return lax.ppermute(block, axis, route)  18.4 us
    unnamed x30, local copies, waits for them, and re-layouts  5.64 us
  transfers between devices with their start and end apart: 7, of which 6 were waited for; matrix products, arithmetic and copies ran while one was open for 5% of the time, Pallas kernels for 0%

commit v1 on v0

--- a/solution.py
+++ b/solution.py
@@ -129,7 +129,8 @@
     value_total = frame_grads[1] + carried[1]
     column_sums = jnp.sum(value_total, axis=0)
     local_table = jnp.where(matches[:, None], column_sums[None, :], 0.0)
-    grad_table = lax.psum(local_table, ("tm", "row"))
+    half = lax.psum(local_table, "row")
+    grad_table = lax.psum(half, "tm")
     return (
         out_full.astype(jnp.bfloat16),
         grad_query.astype(jnp.bfloat16),

time: 187 us -> 169 us (0.904)
  blocking collectives: 60 us -> 42.1 us
    psum x1 -> x2, blocking collectives: 57.6 us -> 39.7 us  [the longest x1 36.3 us: on_device(): grad_table = lax.psum(half, 'tm')]
where the time goes in v1:
time: 169 us
  waiting for transfers between devices  62.6 us (37%)
  blocking collectives  42.1 us (25%)
  between operations  19 us (11%)
  starting transfers between devices  18.4 us (11%)
  local copies, waits for them, and re-layouts  11.9 us (7%)
  other arithmetic  10 us (6%)
  matrix products  4.76 us (3%)
    ppermute x6, waiting for transfers between devices, from_behind(): return lax.ppermute(block, axis, route)  62.6 us
    psum x1, blocking collectives, on_device(): grad_table = lax.psum(half, 'tm')  36.3 us
    ppermute x6, starting transfers between devices, from_behind(): return lax.ppermute(block, axis, route)  18.4 us
    unnamed x30, local copies, waits for them, and re-layouts  5.63 us
    psum x1, blocking collectives, on_device(): half = lax.psum(local_table, 'row')  3.4 us
  transfers between devices with their start and end apart: 7, of which 6 were waited for; matrix products, arithmetic and copies ran while one was open for 5% of the time, Pallas kernels for 0%

profile of v1, /device:TPU:0, one launch (start us, length us, event | category | flops | bytes accessed | tf_op | source)
XLA Modules:
  0.0 168.8 jit_solution(17642917675835152370)
XLA Ops:
  10.1 4.9 %collective-permute-start = (bf16[2,128,768]{2,1,0:T(8,128)(2,1)S(1)}, bf16[2,128,768]{2,1,0:T(8,128)(2,1)S(1)}, u32[]{:S(2)}, u32[]{:S(2)}) collective-permute-start(bf16[2,128,768]{2,1,0:T(8,128)(2,1)S(1)} %pad_maximum_fusion.10), channel_id=1, source_target_pairs={{0,2},{2,4},{4,6},{6,8},{8,10},{10,12},{12,14},{1,3},{3,5},{5,7},{... | collective-permute-start | bytes 1179656 | tf_op jit(solution)/shard_map/ppermute | solution.py:16
  16.4 6.9 %collective-permute-done = bf16[2,128,768]{2,1,0:T(8,128)(2,1)S(1)} collective-permute-done((bf16[2,128,768]{2,1,0:T(8,128)(2,1)S(1)}, bf16[2,128,768]{2,1,0:T(8,128)(2,1)S(1)}, u32[]{:S(2)}, u32[]{:S(2)}) %collective-permute-start) | collective-permute-done | bytes 393248 | tf_op jit(solution)/shard_map/ppermute | solution.py:16
  23.3 4.4 %collective-permute-start.1 = (bf16[2,128,768]{2,1,0:T(8,128)(2,1)S(1)}, bf16[2,128,768]{2,1,0:T(8,128)(2,1)S(1)}, u32[]{:S(2)}, u32[]{:S(2)}) collective-permute-start(bf16[2,128,768]{2,1,0:T(8,128)(2,1)S(1)} %collective-permute-done), channel_id=1, source_target_pairs={{0,2},{2,4},{4,6},{6,8},{8,10},{10,12},{12,14},{1,3},{3,5},{5,7},{... | collective-permute-start | bytes 1179656 | tf_op jit(solution)/shard_map/ppermute | solution.py:16
  27.7 2.4 %all_gather.3 = bf16[2,256,768]{2,1,0:T(8,128)(2,1)S(1)} all-gather(bf16[2,128,768]{2,1,0:T(8,128)(2,1)S(1)} %pad_maximum_fusion.10), channel_id=1, replica_groups=mesh['grp'=2,'tm'=8,'row'=2] {'row'}, dimensions={1}, use_global_device_ids=true | all-gather | bytes 1179648 | tf_op jit(solution)/shard_map/all_gather | solution.py:83
  30.1 5.0 %collective-permute-done.1 = bf16[2,128,768]{2,1,0:T(8,128)(2,1)S(1)} collective-permute-done((bf16[2,128,768]{2,1,0:T(8,128)(2,1)S(1)}, bf16[2,128,768]{2,1,0:T(8,128)(2,1)S(1)}, u32[]{:S(2)}, u32[]{:S(2)}) %collective-permute-start.1) | collective-permute-done | bytes 393248 | tf_op jit(solution)/shard_map/ppermute | solution.py:16
  35.2 5.1 %collective-permute-start.2 = (bf16[2,128,768]{2,1,0:T(8,128)(2,1)S(1)}, bf16[2,128,768]{2,1,0:T(8,128)(2,1)}, u32[]{:S(2)}, u32[]{:S(2)}) collective-permute-start(bf16[2,128,768]{2,1,0:T(8,128)(2,1)S(1)} %collective-permute-done.1), channel_id=1, source_target_pairs={{0,2},{2,4},{4,6},{6,8},{8,10},{10,12},{12,14},{1,3},{3,5},{5,7},{... | collective-permute-start | bytes 1179656 | tf_op jit(solution)/shard_map/ppermute | solution.py:16
  43.7 2.4 %collective-permute-done.2 = bf16[2,128,768]{2,1,0:T(8,128)(2,1)} collective-permute-done((bf16[2,128,768]{2,1,0:T(8,128)(2,1)S(1)}, bf16[2,128,768]{2,1,0:T(8,128)(2,1)}, u32[]{:S(2)}, u32[]{:S(2)}) %collective-permute-start.2) | collective-permute-done | bytes 393248 | tf_op jit(solution)/shard_map/ppermute | solution.py:16
  46.1 1.1 pad_maximum_fusion.1
  50.8 1.6 convolution_bitcast_fusion
  52.5 1.1 multiply_reduce_fusion
  55.7 1.0 fusion.27
  57.6 1.3 pad_maximum_fusion
  58.9 1.4 copy-done.2
  61.2 1.3 collective-permute-start.3
  63.8 17.5 %collective-permute-done.3 = f32[2,128,768]{2,1,0:T(8,128)S(1)} collective-permute-done((f32[2,128,768]{2,1,0:T(8,128)S(1)}, f32[2,128,768]{2,1,0:T(8,128)S(1)}, u32[]{:S(2)}, u32[]{:S(2)}) %collective-permute-start.3) | collective-permute-done | bytes 786464 | tf_op jit(solution)/shard_map/ppermute | solution.py:16
  81.5 1.4 collective-permute-start.4
  84.2 17.0 %collective-permute-done.4 = f32[2,128,768]{2,1,0:T(8,128)S(1)} collective-permute-done((f32[2,128,768]{2,1,0:T(8,128)S(1)}, f32[2,128,768]{2,1,0:T(8,128)S(1)}, u32[]{:S(2)}, u32[]{:S(2)}) %collective-permute-start.4) | collective-permute-done | bytes 786464 | tf_op jit(solution)/shard_map/ppermute | solution.py:16
  101.1 1.0 add_add_fusion
  102.2 1.3 collective-permute-start.5
  103.5 1.7 %copy.47 = bf16[128,768]{1,0:T(8,128)(2,1)} copy(bf16[128,768]{0,1:T(8,128)(2,1)} %bitcast.99) | data formatting | bytes 393216
  106.4 13.7 %collective-permute-done.5 = f32[2,128,768]{2,1,0:T(8,128)S(1)} collective-permute-done((f32[2,128,768]{2,1,0:T(8,128)}, f32[2,128,768]{2,1,0:T(8,128)S(1)}, u32[]{:S(2)}, u32[]{:S(2)}) %collective-permute-start.5) | collective-permute-done | bytes 786464 | tf_op jit(solution)/shard_map/ppermute | solution.py:16
  120.2 2.0 %fusion.16 = (f32[768]{0:T(1024)S(1)}, bf16[128,768]{1,0:T(8,128)(2,1)}, bf16[128,768]{1,0:T(8,128)(2,1)}) fusion(f32[2,128,768]{2,1,0:T(8,128)S(1)} %collective-permute-done.5, f32[2,128,768]{2,1,0:T(8,128)} %reduce-scatter.2.cloned.1.call-done), kind=kLoop, calls=%fused_computation.41 | loop fusion | flops 490752 | bytes 1969152 | tf_op jit(solution)/shard_map/reduce_sum | solution.py:130
  122.2 3.4 %psum.14 = f32[8,768]{1,0:T(8,128)S(1)} all-reduce(f32[8,768]{1,0:T(8,128)S(1)} %broadcast_select_fusion.1), channel_id=1, replica_groups=mesh['grp'=2,'tm'=8,'row'=2] {'row'}, use_global_device_ids=true, to_apply=%region_5.6 | all-reduce | flops 6144 | bytes 49152 | tf_op jit(solution)/shard_map/psum | solution.py:132
  125.6 36.3 %psum.15 = f32[8,768]{1,0:T(8,128)} all-reduce(f32[8,768]{1,0:T(8,128)S(1)} %psum.14), channel_id=1, replica_groups=mesh['grp'=2,'tm'=8,'row'=2] {'tm'}, use_global_device_ids=true, to_apply=%region_6.7 | all-reduce | flops 6144 | bytes 49152 | tf_op jit(solution)/shard_map/psum | solution.py:133
  (69 shorter events, 14.5 us)
Async XLA Ops:
  7.2 0.8 copy-start
  7.2 33.1 %copy-start.12 = (s32[1,2]{1,0:T(1,128)S(1)}, s32[1,2]{1,0:T(1,128)}, u32[]{:S(2)}) copy-start(s32[1,2]{1,0:T(1,128)} %param.13) | copy-start | bytes 28
  7.2 35.0 %copy-start.10 = (bf16[128,768]{1,0:T(8,128)(2,1)S(1)}, bf16[128,768]{1,0:T(8,128)(2,1)}, u32[]{:S(2)}) copy-start(bf16[128,768]{1,0:T(8,128)(2,1)} %param.7) | copy-start | bytes 589828
  7.2 113.0 %reduce-scatter.2.cloned.1.call-start = ((), (), s32[]{:S(2)}) async-start(), calls=%async_computation.1 | async-start | bytes 2359296 | tf_op jit(solution)/shard_map/reduce_scatter | solution.py:107
  8.1 34.3 %copy-start.11 = (bf16[128,768]{1,0:T(8,128)(2,1)S(1)}, bf16[128,768]{1,0:T(8,128)(2,1)}, u32[]{:S(2)}) copy-start(bf16[128,768]{1,0:T(8,128)(2,1)} %param.10) | copy-start | bytes 589828
  10.1 13.2 %collective-permute-start = (bf16[2,128,768]{2,1,0:T(8,128)(2,1)S(1)}, bf16[2,128,768]{2,1,0:T(8,128)(2,1)S(1)}, u32[]{:S(2)}, u32[]{:S(2)}) collective-permute-start(bf16[2,128,768]{2,1,0:T(8,128)(2,1)S(1)} %pad_maximum_fusion.10), channel_id=1, source_target_pairs={{0,2},{2,4},{4,6},{6,8},{8,10},{10,12},{12,14},{1,3},{3,5},{5,7},{... | collective-permute-start | bytes 1179656 | tf_op jit(solution)/shard_map/ppermute | solution.py:16
  23.3 11.9 %collective-permute-start.1 = (bf16[2,128,768]{2,1,0:T(8,128)(2,1)S(1)}, bf16[2,128,768]{2,1,0:T(8,128)(2,1)S(1)}, u32[]{:S(2)}, u32[]{:S(2)}) collective-permute-start(bf16[2,128,768]{2,1,0:T(8,128)(2,1)S(1)} %collective-permute-done), channel_id=1, source_target_pairs={{0,2},{2,4},{4,6},{6,8},{8,10},{10,12},{12,14},{1,3},{3,5},{5,7},{... | collective-permute-start | bytes 1179656 | tf_op jit(solution)/shard_map/ppermute | solution.py:16
  35.2 10.9 %collective-permute-start.2 = (bf16[2,128,768]{2,1,0:T(8,128)(2,1)S(1)}, bf16[2,128,768]{2,1,0:T(8,128)(2,1)}, u32[]{:S(2)}, u32[]{:S(2)}) collective-permute-start(bf16[2,128,768]{2,1,0:T(8,128)(2,1)S(1)} %collective-permute-done.1), channel_id=1, source_target_pairs={{0,2},{2,4},{4,6},{6,8},{8,10},{10,12},{12,14},{1,3},{3,5},{5,7},{... | collective-permute-start | bytes 1179656 | tf_op jit(solution)/shard_map/ppermute | solution.py:16
  48.7 1.2 copy-start.3
  50.8 1.7 copy-start.9
  54.1 1.0 copy-start.7
  55.6 1.7 %copy-start.1 = (f32[512,8,96]{0,2,1:T(8,128)S(1)}, f32[512,8,96]{0,2,1:T(8,128)}, u32[]{:S(2)}) copy-start(f32[512,8,96]{0,2,1:T(8,128)} %convolution_bitcast_fusion) | copy-start | bytes 4718596
  58.9 1.4 copy-start.2
  58.9 1.5 copy-start.6
  58.9 1.7 copy-start.5
  61.2 20.1 %collective-permute-start.3 = (f32[2,128,768]{2,1,0:T(8,128)S(1)}, f32[2,128,768]{2,1,0:T(8,128)S(1)}, u32[]{:S(2)}, u32[]{:S(2)}) collective-permute-start(f32[2,128,768]{2,1,0:T(8,128)S(1)} %select_add_fusion), channel_id=1, source_target_pairs={{2,0},{4,2},{6,4},{8,6},{10,8},{12,10},{14,12},{3,1},{5,3},{7,5},{... | collective-permute-start | bytes 2359304 | tf_op jit(solution)/shard_map/ppermute | solution.py:16
  81.4 23.8 %copy-start.4 = (bf16[256,8,96]{0,2,1:T(8,128)(2,1)S(1)}, bf16[256,8,96]{0,2,1:T(8,128)(2,1)}, u32[]{:S(2)}) copy-start(bf16[256,8,96]{0,2,1:T(8,128)(2,1)} %copy-done.3) | copy-start | bytes 1179652
  81.4 23.8 %copy-start.8 = (bf16[8,128,512]{1,2,0:T(8,128)(2,1)S(1)}, bf16[8,128,512]{1,2,0:T(8,128)(2,1)}, u32[]{:S(2)}) copy-start(bf16[8,128,512]{1,2,0:T(8,128)(2,1)} %copy-done.7) | copy-start | bytes 3145732
  81.5 19.7 %collective-permute-start.4 = (f32[2,128,768]{2,1,0:T(8,128)S(1)}, f32[2,128,768]{2,1,0:T(8,128)S(1)}, u32[]{:S(2)}, u32[]{:S(2)}) collective-permute-start(f32[2,128,768]{2,1,0:T(8,128)S(1)} %add_add_fusion.1), channel_id=1, source_target_pairs={{2,0},{4,2},{6,4},{8,6},{10,8},{12,10},{14,12},{3,1},{5,3},{7,5},{... | collective-permute-start | bytes 2359304 | tf_op jit(solution)/shard_map/ppermute | solution.py:16
  102.2 18.0 %collective-permute-start.5 = (f32[2,128,768]{2,1,0:T(8,128)}, f32[2,128,768]{2,1,0:T(8,128)S(1)}, u32[]{:S(2)}, u32[]{:S(2)}) collective-permute-start(f32[2,128,768]{2,1,0:T(8,128)} %add_add_fusion), channel_id=1, source_target_pairs={{2,0},{4,2},{6,4},{8,6},{10,8},{12,10},{14,12},{3,1},{5,3},{7,5},{... | collective-permute-start | bytes 2359304 | tf_op jit(solution)/shard_map/ppermute | solution.py:16
Sparse Core Ops, SparseCore 0:
  59.1 13.1 reduce-scatter.1
